TPU v7x, 32 devices: a whole 2x2x4 slice. The times are simulated.
32 devices in a mesh: fsdp: 4 (over x, core), tok: 8 (over z, y).
Axes of the slice: x: 2, y: 2, z: 4, core: 2. Of those that a mesh axis runs over, the one named last changes fastest.
Arguments:
- states: bfloat16 [4, 512, 1024], P('fsdp', 'tok'), may hold values from -8 to 8
- cache_keys: bfloat16 [4, 1024, 1024], P('fsdp', 'tok'), may hold values from -6 to 6
- cache_values: bfloat16 [4, 1024, 1024], P('fsdp', 'tok'), may hold values from -6 to 6
- cache_len: int32 [4], P('fsdp'), may hold values from 1 to 1024, as said below
- token_slot: int32 [4, 512], P('fsdp', 'tok'), may hold values from 0 to 511, as said below
- bucket_table: int32 [1536], replicated, may hold values from 0 to 31
- rel_bias: float32 [32, 16], replicated, may hold values from -3 to 250
- norm_gain: float32 [1024], replicated, may hold values from 0.5 to 1.5
- w_query: bfloat16 [1024, 1024], P(('fsdp', 'tok')), may hold values from -0.0234375 to 0.0234375
- w_key: bfloat16 [1024, 1024], P(('fsdp', 'tok')), may hold values from -0.1875 to 0.1875
- w_value: bfloat16 [1024, 1024], P(('fsdp', 'tok')), may hold values from -0.1875 to 0.1875
- w_out: bfloat16 [1024, 1024], P(('fsdp', 'tok')), may hold values from -1.5 to 1.5
Outputs:
- hidden_out: bfloat16 [4, 512, 1024], P('fsdp', 'tok')
- new_keys: bfloat16 [4, 512, 1024], P('fsdp', 'tok')
- new_values: bfloat16 [4, 512, 1024], P('fsdp', 'tok')
Inputs may be any that keep to these rules, and one draw needn't show every extreme that they name: `cache_len`: one request has exactly 1024 live rows. `token_slot`: each row is a permutation of 0 to 511; every aligned block of 64 tokens of a request has exactly 8 of its slots in each aligned block of 64 slots.
All inputs are finite; a program needn't handle non-finite values.
Results may differ from a plain program's by a relative error of at most 0.0095.
Values may be sent and summed in bfloat16 or wider, within the bound.
No kernel may reach another device: no remote copies, remote signals or barrier semaphores. Data moves between devices by JAX's collectives and lax.ppermute only.
A program may use at most 64 MiB of HBM per device.

v0:
```python
import jax
import jax.numpy as jnp
from jax import lax
from jax.sharding import PartitionSpec as P

far_away = 1073741824
neg_floor = -1e30


def bias_scores(bucket_ids, bias_parts):
    bucket_count = bias_parts[0].shape[0]
    one_hot = (bucket_ids[..., None] == jnp.arange(bucket_count, dtype=jnp.int32)).astype(
        jnp.bfloat16
    )
    high_part = jnp.einsum(
        "qkb,bh->hqk", one_hot, bias_parts[0], preferred_element_type=jnp.float32
    )
    middle = jnp.einsum("qkb,bh->hqk", one_hot, bias_parts[1], preferred_element_type=jnp.float32)
    low_part = jnp.einsum("qkb,bh->hqk", one_hot, bias_parts[2], preferred_element_type=jnp.float32)
    return high_part + middle + low_part


def absorb(running, queries, query_pos, keys_here, values_here, key_pos, bucket_table, bias_parts):
    totals, peak_old, masses = running
    head_count = queries.shape[1]
    keys_split = keys_here.reshape(keys_here.shape[0], head_count, -1)
    values_split = values_here.reshape(values_here.shape[0], head_count, -1)
    scores = jnp.einsum("qhd,khd->hqk", queries, keys_split, preferred_element_type=jnp.float32)
    distance = query_pos[:, None] - key_pos[None, :]
    allowed = (distance >= 0)[None]
    bucket_ids = jnp.take(bucket_table, jnp.clip(distance, 0, bucket_table.shape[0] - 1), axis=0)
    scores = scores + bias_scores(bucket_ids, bias_parts)
    new_peak = jnp.maximum(peak_old, jnp.max(jnp.where(allowed, scores, neg_floor), axis=-1))
    weights = jnp.where(allowed, jnp.exp(scores - new_peak[..., None]), 0.0)
    shrink = jnp.exp(peak_old - new_peak)
    masses = masses * shrink + jnp.sum(weights, axis=-1)
    totals = totals * jnp.transpose(shrink)[..., None] + jnp.einsum(
        "hqk,khd->qhd",
        weights.astype(jnp.bfloat16),
        values_split,
        preferred_element_type=jnp.float32,
    )
    return (totals, new_peak, masses)


def permute_rows(selector, rows):
    return jnp.dot(selector.astype(jnp.bfloat16), rows, preferred_element_type=jnp.float32).astype(
        jnp.bfloat16
    )


def permute_ints(selector, values):
    return jnp.sum(jnp.where(selector, values[None, :], 0), axis=1).astype(jnp.int32)


def shards(
    states,
    cache_keys,
    cache_values,
    cache_len,
    token_slot,
    bucket_table,
    rel_bias,
    norm_gain,
    w_query,
    w_key,
    w_value,
    w_out,
):
    peer_count = lax.axis_size("tok")
    my_index = lax.axis_index("tok")
    tokens = states[0]
    tok_rows = tokens.shape[0]
    feature_count = tokens.shape[1]
    per_peer = tok_rows // peer_count
    head_count = rel_bias.shape[1]
    head_size = feature_count // head_count
    slot_ids = token_slot[0]
    length = cache_len[0]
    row_iota = jnp.arange(tok_rows, dtype=jnp.int32)
    ranking = jnp.sum((slot_ids[None, :] < slot_ids[:, None]).astype(jnp.int32), axis=1)
    sort_sel = ranking[None, :] == row_iota[:, None]
    sent_rows = permute_rows(sort_sel, tokens).reshape(peer_count, per_peer, feature_count)
    sent_slots = permute_ints(sort_sel, slot_ids).reshape(peer_count, per_peer)
    sent_pos = (my_index * tok_rows + permute_ints(sort_sel, row_iota)).reshape(
        peer_count, per_peer
    )
    got_rows, got_slots, got_pos = (
        lax.all_to_all(sent_rows, "tok", split_axis=0, concat_axis=0, tiled=True),
        lax.all_to_all(sent_slots, "tok", split_axis=0, concat_axis=0, tiled=True),
        lax.all_to_all(sent_pos, "tok", split_axis=0, concat_axis=0, tiled=True),
    )
    local_slot = got_slots.reshape(tok_rows) - my_index * tok_rows
    place_sel = local_slot[None, :] == row_iota[:, None]
    dealt = permute_rows(place_sel, got_rows.reshape(tok_rows, feature_count))
    dealt_pos = permute_ints(place_sel, got_pos.reshape(tok_rows))
    query_w, key_w, value_w, out_w = (
        lax.all_gather(w_query, ("fsdp", "tok"), axis=0, tiled=True),
        lax.all_gather(w_key, ("fsdp", "tok"), axis=0, tiled=True),
        lax.all_gather(w_value, ("fsdp", "tok"), axis=0, tiled=True),
        lax.all_gather(w_out, ("fsdp", "tok"), axis=0, tiled=True),
    )
    wide_in = dealt.astype(jnp.float32)
    inverse = lax.rsqrt(jnp.mean(wide_in * wide_in, axis=-1, keepdims=True) + 1e-06)
    normed = (wide_in * inverse * norm_gain).astype(jnp.bfloat16)
    queries = jnp.dot(normed, query_w, preferred_element_type=jnp.float32).astype(jnp.bfloat16)
    new_keys = jnp.dot(normed, key_w, preferred_element_type=jnp.float32).astype(jnp.bfloat16)
    new_values = jnp.dot(normed, value_w, preferred_element_type=jnp.float32).astype(jnp.bfloat16)
    query_pos = length + dealt_pos
    cache_rows = cache_keys.shape[1]
    cache_spot = my_index * cache_rows + jnp.arange(cache_rows, dtype=jnp.int32)
    key_pos = jnp.concatenate([jnp.where(cache_spot < length, cache_spot, far_away), query_pos])
    keys_here = jnp.concatenate([cache_keys[0], new_keys])
    values_here = jnp.concatenate([cache_values[0], new_values])
    bias_high = rel_bias.astype(jnp.bfloat16)
    remainder = rel_bias - bias_high.astype(jnp.float32)
    bias_middle = remainder.astype(jnp.bfloat16)
    bias_low = (remainder - bias_middle.astype(jnp.float32)).astype(jnp.bfloat16)
    bias_parts = (bias_high, bias_middle, bias_low)
    query_heads = queries.reshape(tok_rows, head_count, head_size)
    shard_len = keys_here.shape[0]
    initial = (
        jnp.zeros((tok_rows, head_count, head_size), jnp.float32),
        jnp.full((head_count, tok_rows), neg_floor, jnp.float32),
        jnp.zeros((head_count, tok_rows), jnp.float32),
    )
    running = initial
    part_keys = lax.all_gather(keys_here, "tok", axis=0, tiled=True)
    part_values = lax.all_gather(values_here, "tok", axis=0, tiled=True)
    part_pos = lax.all_gather(key_pos, "tok", axis=0, tiled=True)
    rows_in = part_keys.shape[0]
    block_len = 2 * shard_len
    shard_count = rows_in // block_len
    blocks = (
        part_keys.reshape(shard_count, block_len, feature_count),
        part_values.reshape(shard_count, block_len, feature_count),
        part_pos.reshape(shard_count, block_len),
    )

    def advance(running_in, block_set):
        return (
            absorb(
                running_in,
                query_heads,
                query_pos,
                block_set[0],
                block_set[1],
                block_set[2],
                bucket_table,
                bias_parts,
            ),
            None,
        )

    running, unused = lax.scan(advance, running, blocks)
    totals, peaks, masses = running
    context = (
        (totals / jnp.transpose(masses)[..., None])
        .reshape(tok_rows, feature_count)
        .astype(jnp.bfloat16)
    )
    result_dealt = (wide_in + jnp.dot(context, out_w, preferred_element_type=jnp.float32)).astype(
        jnp.bfloat16
    )
    back_rows = permute_rows(jnp.transpose(place_sel), result_dealt).reshape(
        peer_count, per_peer, feature_count
    )
    returned = lax.all_to_all(back_rows, "tok", split_axis=0, concat_axis=0, tiled=True)
    hidden = permute_rows(jnp.transpose(sort_sel), returned.reshape(tok_rows, feature_count))
    return (hidden[None], new_keys[None], new_values[None])


def solution(mesh):
    in_specs = (
        P("fsdp", "tok", None),
        P("fsdp", "tok", None),
        P("fsdp", "tok", None),
        P("fsdp"),
        P("fsdp", "tok"),
        P(),
        P(),
        P(),
        P(("fsdp", "tok"), None),
        P(("fsdp", "tok"), None),
        P(("fsdp", "tok"), None),
        P(("fsdp", "tok"), None),
    )
    out_specs = (P("fsdp", "tok", None), P("fsdp", "tok", None), P("fsdp", "tok", None))
    return jax.shard_map(shards, mesh=mesh, in_specs=in_specs, out_specs=out_specs, check_vma=False)
```

profile of v0, /device:TPU:0, one launch (start us, length us, event | category | flops | bytes accessed | tf_op | source)
XLA Modules:
  0.0 936.9 jit_solution(472488924100509051)
XLA Ops:
  9.4 0.9 convert_reduce_fusion
  11.8 7.3 all-to-all-start
  19.9 5.6 all-to-all-done
  25.4 3.4 all-to-all-start.1
  29.0 7.2 all-to-all-done.1
  38.0 32.8 %all-gather.13.cloned.1.call-done = bf16[1024,1024]{1,0:T(8,128)(2,1)} async-done(((bf16[32,1024]{1,0:T(8,128)(2,1)}), bf16[1024,1024]{1,0:T(8,128)(2,1)}) %all-gather.13.cloned.1.call-update) | async-done | bytes 2097168 | tf_op jit(solution)/shard_map/all_gather | solution.py:100
  70.8 2.1 convolution_convert_fusion.2
  74.4 54.8 %all-gather.7.cloned.1.call-done = bf16[1024,1024]{1,0:T(8,128)(2,1)} async-done(((bf16[32,1024]{1,0:T(8,128)(2,1)}), bf16[1024,1024]{1,0:T(8,128)(2,1)}) %all-gather.7.cloned.1.call-update) | async-done | bytes 2097168 | tf_op jit(solution)/shard_map/all_gather | solution.py:99
  129.2 2.1 convolution_convert_fusion.4
  133.4 4.4 all-to-all-start.2
  140.4 3.7 all-to-all-done.2
  145.7 8.7 all-reduce
  154.4 33.1 %all-gather.11.cloned.1.call-done = bf16[1024,1024]{1,0:T(8,128)(2,1)} async-done(((bf16[32,1024]{1,0:T(8,128)(2,1)}), bf16[1024,1024]{1,0:T(8,128)(2,1)}) %all-gather.11.cloned.1.call-update) | async-done | bytes 2097168 | tf_op jit(solution)/shard_map/all_gather | solution.py:98
  187.6 2.1 convolution_convert_fusion.3
  190.6 58.3 %all-gather.15.cloned.1.call-done = bf16[1536,1024]{1,0:T(8,128)(2,1)} async-done(((bf16[192,1024]{1,0:T(8,128)(2,1)}), bf16[1536,1024]{1,0:T(8,128)(2,1)}) %all-gather.15.cloned.1.call-update) | async-done | bytes 3145744 | tf_op jit(solution)/shard_map/all_gather | solution.py:129
  249.0 61.1 %all-gather.9.cloned.1.call-done = bf16[1536,1024]{1,0:T(8,128)(2,1)} async-done(((bf16[192,1024]{1,0:T(8,128)(2,1)}), bf16[1536,1024]{1,0:T(8,128)(2,1)}) %all-gather.9.cloned.1.call-update) | async-done | bytes 3145744 | tf_op jit(solution)/shard_map/all_gather | solution.py:128
  310.1 605.3 %while.15 = (s32[]{:T(128)}, f32[64,16,64]{0,2,1:T(8,128)}, f32[16,64]{1,0:T(8,128)S(1)}, f32[16,64]{1,0:T(8,128)S(1)}, s32[64]{0:T(128)S(1)}, /*index=5*/s32[4,...) while((s32[]{:T(128)}, f32[64,16,64]{0,2,1:T(8,128)}, ...), condition=%wide.region_8.9_spmd.clone, body=%wide.region_5.8_spmd.clone.sunk | while | flops 183465984 | bytes 27471288 | solution.py:155
  310.3 135.5 %gather_fusion = s32[24576]{0:T(1024)S(1)} fusion(s32[1536]{0:T(1024)S(1)} %get-tuple-element.335, s32[24576]{0:T(1024)S(1)} %broadcast_clamp_fusion.2), kind=kCustom, calls=%fused_computation.clone.clone.1 | custom fusion | bytes 294912 | tf_op jit(solution)/shard_map/while/body/eval_jaxpr/jit(_take)/gather | solution.py:31
  446.5 1.8 fusion.71
  448.3 1.7 fusion.72
  450.1 2.4 constant_dynamic-slice_fusion.3
  452.5 1.2 copy.53
  453.7 4.1 select_reduce_fusion.5
  459.3 1.3 fusion.74
  460.8 135.5 %gather_fusion = s32[24576]{0:T(1024)S(1)} fusion(s32[1536]{0:T(1024)S(1)} %get-tuple-element.335, s32[24576]{0:T(1024)S(1)} %broadcast_clamp_fusion.2), kind=kCustom, calls=%fused_computation.clone.clone.1 | custom fusion | bytes 294912 | tf_op jit(solution)/shard_map/while/body/eval_jaxpr/jit(_take)/gather | solution.py:31
  597.1 1.8 fusion.71
  598.9 1.7 fusion.72
  600.7 2.4 constant_dynamic-slice_fusion.3
  603.1 1.2 copy.53
  604.2 4.1 select_reduce_fusion.5
  609.8 2.4 fusion.74
  612.4 135.5 %gather_fusion = s32[24576]{0:T(1024)S(1)} fusion(s32[1536]{0:T(1024)S(1)} %get-tuple-element.335, s32[24576]{0:T(1024)S(1)} %broadcast_clamp_fusion.2), kind=kCustom, calls=%fused_computation.clone.clone.1 | custom fusion | bytes 294912 | tf_op jit(solution)/shard_map/while/body/eval_jaxpr/jit(_take)/gather | solution.py:31
  748.7 1.8 fusion.71
  750.4 1.7 fusion.72
  752.3 2.4 constant_dynamic-slice_fusion.3
  754.6 1.2 copy.53
  755.8 4.1 select_reduce_fusion.5
  761.4 2.4 fusion.74
  764.0 135.5 %gather_fusion = s32[24576]{0:T(1024)S(1)} fusion(s32[1536]{0:T(1024)S(1)} %get-tuple-element.335, s32[24576]{0:T(1024)S(1)} %broadcast_clamp_fusion.2), kind=kCustom, calls=%fused_computation.clone.clone.1 | custom fusion | bytes 294912 | tf_op jit(solution)/shard_map/while/body/eval_jaxpr/jit(_take)/gather | solution.py:31
  900.3 1.8 fusion.71
  902.0 1.7 fusion.72
  903.9 2.4 constant_dynamic-slice_fusion.3
  906.2 1.2 copy.53
  907.4 4.1 select_reduce_fusion.5
  913.0 2.4 fusion.74
  915.4 1.1 divide_convert_fusion
  916.6 2.2 fusion.25
  918.8 10.4 %all_to_all.25 = bf16[8,8,1024]{2,1,0:T(8,128)(2,1)S(1)} all-to-all(bf16[8,8,1024]{2,1,0:T(8,128)(2,1)S(1)} %fusion.25), channel_id=1, replica_groups=mesh['fsdp'=4,'tok'=8] {'tok'}, dimensions={0} | all-to-all | bytes 262144 | tf_op jit(solution)/shard_map/all_to_all | solution.py:168
  (128 shorter events, 24.2 us)
Async XLA Ops:
  7.2 11.9 %copy-start = (bf16[1,64,1024]{2,1,0:T(8,128)(2,1)S(1)}, bf16[1,64,1024]{2,1,0:T(8,128)(2,1)}, u32[]{:S(2)}) copy-start(bf16[1,64,1024]{2,1,0:T(8,128)(2,1)} %param.14) | copy-start | bytes 393220
  7.2 63.6 %all-gather.13.cloned.1.call-start = ((), (), s32[]{:S(2)}) async-start(), calls=%async_computation.7 | async-start | bytes 2162688 | tf_op jit(solution)/shard_map/all_gather | solution.py:100
  7.9 121.3 %all-gather.7.cloned.1.call-start = ((), (), s32[]{:S(2)}) async-start(), calls=%async_computation.4 | async-start | bytes 2162688 | tf_op jit(solution)/shard_map/all_gather | solution.py:99
  8.7 178.9 %all-gather.11.cloned.1.call-start = ((), (), s32[]{:S(2)}) async-start(), calls=%async_computation.6 | async-start | bytes 2162688 | tf_op jit(solution)/shard_map/all_gather | solution.py:98
  10.3 15.1 %copy-start.11 = (s32[64]{0:T(128)}, s32[64]{0:T(128)S(1)}, u32[]{:S(2)}) copy-start(s32[64]{0:T(128)S(1)} %convert_reduce_fusion) | copy-start | bytes 772
  11.8 13.7 %all-to-all-start = ((s32[8,1,8]{2,1,0:T(1,128)}), s32[8,1,8]{2,1,0:T(1,128)S(1)}, u32[]{:S(2)}, u32[]{:S(2)}) async-start(s32[8,1,8]{2,1,0:T(1,128)} %bitcast.1), calls=%async_computation | async-start | bytes 8192 | tf_op jit(solution)/shard_map/all_to_all | solution.py:90
  25.4 10.8 %all-to-all-start.1 = ((bf16[8,8,1024]{2,1,0:T(8,128)(2,1)}), bf16[8,8,1024]{2,1,0:T(8,128)(2,1)S(1)}, u32[]{:S(2)}, u32[]{:S(2)}) async-start(bf16[8,8,1024]{2,1,0:T(8,128)(2,1)} %fusion.26), calls=%async_computation.1 | async-start | bytes 262144 | tf_op jit(solution)/shard_map/all_to_all | solution.py:89
  28.8 220.1 %all-gather.15.cloned.1.call-start = ((), (), s32[]{:S(2)}) async-start(), calls=%async_computation.8 | async-start | bytes 3538944 | tf_op jit(solution)/shard_map/all_gather | solution.py:129
  29.0 116.4 %copy-start.9 = (s32[64]{0:T(128)}, s32[64]{0:T(128)S(1)}, u32[]{:S(2)}) copy-start(s32[64]{0:T(128)S(1)} %sub.69) | copy-start | bytes 772
  29.0 44.5 %copy-start.6 = (bf16[1,128,1024]{2,1,0:T(8,128)(2,1)S(1)}, bf16[1,128,1024]{2,1,0:T(8,128)(2,1)}, u32[]{:S(2)}) copy-start(bf16[1,128,1024]{2,1,0:T(8,128)(2,1)} %param.16) | copy-start | bytes 786436
  36.5 0.7 copy-start.3
  72.9 0.7 copy-start.4
  74.3 57.6 %copy-start.7 = (bf16[1,128,1024]{2,1,0:T(8,128)(2,1)S(1)}, bf16[1,128,1024]{2,1,0:T(8,128)(2,1)}, u32[]{:S(2)}) copy-start(bf16[1,128,1024]{2,1,0:T(8,128)(2,1)} %param.15) | copy-start | bytes 786436
  74.3 64.7 %copy-start.8 = (f32[32,16]{0,1:T(8,128)S(1)}, f32[32,16]{0,1:T(8,128)}, u32[]{:S(2)}) copy-start(f32[32,16]{0,1:T(8,128)} %param.20) | copy-start | bytes 6148
  74.3 64.7 %copy-start.13 = (u32[32]{0:T(128)S(1)}, u32[32]{0:T(128)}, u32[]{:S(2)}) copy-start(u32[32]{0:T(128)} %constant.64) | copy-start | bytes 388
  74.4 235.7 %all-gather.9.cloned.1.call-start = ((), (), s32[]{:S(2)}) async-start(), calls=%async_computation.5 | async-start | bytes 3538944 | tf_op jit(solution)/shard_map/all_gather | solution.py:128
  131.3 0.7 copy-start.5
  133.4 10.8 %all-to-all-start.2 = ((s32[8,1,8]{2,1,0:T(1,128)}), s32[8,1,8]{2,1,0:T(1,128)S(1)}, u32[]{:S(2)}, u32[]{:S(2)}) async-start(s32[8,1,8]{2,1,0:T(1,128)} %bitcast.6), calls=%async_computation.2 | async-start | bytes 8192 | tf_op jit(solution)/shard_map/all_to_all | solution.py:91
  137.8 778.8 %all-gather.17.cloned.1.call-start = ((), (), s32[]{:S(2)}) async-start(), calls=%async_computation.9 | async-start | bytes 2162688 | tf_op jit(solution)/shard_map/all_gather | solution.py:101
  154.4 155.7 %copy-start.1 = (s32[1536]{0:T(1024)S(1)}, s32[1536]{0:T(1024)}, u32[]{:S(2)}) copy-start(s32[1536]{0:T(1024)} %param.19) | copy-start | bytes 18436
  310.1 606.5 %copy-start.10 = (s32[64]{0:T(128)S(1)}, s32[64]{0:T(128)}, u32[]{:S(2)}) copy-start(s32[64]{0:T(128)} %copy-done.9) | copy-start | bytes 772
  457.8 1.2 copy-start.2
  608.3 1.2 copy-start.2
  759.9 1.2 copy-start.2
  911.5 1.2 copy-start.2
  916.5 12.7 %copy-start.12 = (s32[64]{0:T(128)S(1)}, s32[64]{0:T(128)}, u32[]{:S(2)}) copy-start(s32[64]{0:T(128)} %copy-done.11) | copy-start | bytes 772
Sparse Core Ops, SparseCore 0:
  11.0 59.7 all-gather.12
  73.8 55.3 all-gather.6
  132.2 55.3 all-gather.10
  189.6 59.2 all-gather.14
  251.0 59.0 all-gather.8
  312.9 55.1 all-gather.16
where the time goes:
time: 938 us; the launch traced here: 937 us
  local copies, waits for them, and re-layouts  566 us (60%)
  waiting for transfers between devices  259 us (28%)
  matrix products  51.5 us (5%)
  blocking collectives  19.1 us (2%)
  between operations  15.7 us (2%)
  starting transfers between devices  15.3 us (2%)
  other arithmetic  9.68 us (1%)
    gather x8, local copies, waits for them, and re-layouts, absorb(): jnp.take(bucket_table, jnp.clip(distance, 0, bucket_table.shape[0] - 1),...  542 us
    all_gather x1, waiting for transfers between devices, shards(): part_keys = lax.all_gather(keys_here, 'tok', axis=0, tiled=True)  61.1 us
    all_gather x1, waiting for transfers between devices, shards(): part_values = lax.all_gather(values_here, 'tok', axis=0, tiled=True)  58.3 us
    all_gather x1, waiting for transfers between devices, shards(): lax.all_gather(w_key, ('fsdp', 'tok'), axis=0, tiled=True)  54.8 us
    all_gather x1, waiting for transfers between devices, shards(): lax.all_gather(w_query, ('fsdp', 'tok'), axis=0, tiled=True)  33.1 us
    all_gather x1, waiting for transfers between devices, shards(): lax.all_gather(w_value, ('fsdp', 'tok'), axis=0, tiled=True)  32.8 us
  transfers between devices with their start and end apart: 9, of which 8 were waited for; matrix products, arithmetic and copies ran while one was open for 66% of the time, Pallas kernels for 0%

commit v1 on v0

--- a/solution.py
+++ b/solution.py
@@ -125,7 +125,12 @@
         jnp.zeros((head_count, tok_rows), jnp.float32),
     )
     running = initial
-    part_keys = lax.all_gather(keys_here, "tok", axis=0, tiled=True)
+    ring = [keys_here]
+    for hop in range(7):
+        ring.append(lax.ppermute(ring[-1], "tok", [(dev, (dev + 1) % 8) for dev in range(8)]))
+    part_keys = jnp.roll(
+        jnp.concatenate(ring[::-1], axis=0), (lax.axis_index("tok") + 1) * ring[0].shape[0], axis=0
+    )
     part_values = lax.all_gather(values_here, "tok", axis=0, tiled=True)
     part_pos = lax.all_gather(key_pos, "tok", axis=0, tiled=True)
     rows_in = part_keys.shape[0]

time: 938 us -> 899 us (0.958)
  waiting for transfers between devices: 259 us -> 207 us
  local copies, waits for them, and re-layouts: 566 us -> 579 us
    ppermute x0 -> x7, waiting for transfers between devices: none -> 70 us  [shards(): lax.ppermute(ring[-1], 'tok', [(dev, (dev + 1) % 8) for dev in range(8)])]
    all_gather x1 -> x0, waiting for transfers between devices: 61.1 us -> none  [shards(): part_keys = lax.all_gather(keys_here, 'tok', axis=0, tiled=True)]
    all_gather x1, waiting for transfers between devices: 33.1 us -> 0.01 us  [shards(): lax.all_gather(w_query, ('fsdp', 'tok'), axis=0, tiled=True)]
    all_gather x1, waiting for transfers between devices: 58.3 us -> 34.2 us  [shards(): part_values = lax.all_gather(values_here, 'tok', axis=0, tiled=True)]
  transfers between devices with their start and end apart: 9 -> 15, of which waited for: 8 -> 12; matrix products, arithmetic and copies ran while one was open for 66% -> 70% of each run, Pallas kernels for 0% -> 0%
where the time goes in v1:
time: 899 us; the launch traced here: 898 us
  local copies, waits for them, and re-layouts  579 us (64%)
  waiting for transfers between devices  207 us (23%)
  matrix products  45.3 us (5%)
  blocking collectives  22.2 us (2%)
  starting transfers between devices  18.4 us (2%)
  between operations  15.5 us (2%)
  other arithmetic  9.55 us (1%)
    gather x8, local copies, waits for them, and re-layouts, absorb(): jnp.take(bucket_table, jnp.clip(distance, 0, bucket_table.shape[0] - 1),...  542 us
    ppermute x7, waiting for transfers between devices, shards(): lax.ppermute(ring[-1], 'tok', [(dev, (dev + 1) % 8) for dev in range(8)])  70 us
    all_gather x1, waiting for transfers between devices, shards(): lax.all_gather(w_key, ('fsdp', 'tok'), axis=0, tiled=True)  54.8 us
    all_gather x1, waiting for transfers between devices, shards(): part_values = lax.all_gather(values_here, 'tok', axis=0, tiled=True)  34.2 us
    all_gather x1, waiting for transfers between devices, shards(): lax.all_gather(w_value, ('fsdp', 'tok'), axis=0, tiled=True)  32.7 us
    dynamic_slice x16, local copies, waits for them, and re-layouts, shards(): running, unused = lax.scan(advance, running, blocks)  23.4 us
  transfers between devices with their start and end apart: 15, of which 12 were waited for; matrix products, arithmetic and copies ran while one was open for 70% of the time, Pallas kernels for 0%

profile of v1, /device:TPU:0, one launch (start us, length us, event | category | flops | bytes accessed | tf_op | source)
XLA Modules:
  0.0 897.8 jit_solution(18407589133996452013)
XLA Ops:
  11.8 7.3 all-to-all-start
  19.9 5.6 all-to-all-done
  25.5 3.4 all-to-all-start.1
  29.0 7.2 all-to-all-done.1
  38.1 32.7 %all-gather.10.cloned.1.call-done = bf16[1024,1024]{1,0:T(8,128)(2,1)} async-done(((bf16[32,1024]{1,0:T(8,128)(2,1)}), bf16[1024,1024]{1,0:T(8,128)(2,1)}) %all-gather.10.cloned.1.call-update) | async-done | bytes 2097168 | tf_op jit(solution)/shard_map/all_gather | solution.py:100
  70.8 2.1 convolution_convert_fusion.2
  74.4 54.8 %all-gather.6.cloned.1.call-done = bf16[1024,1024]{1,0:T(8,128)(2,1)} async-done(((bf16[32,1024]{1,0:T(8,128)(2,1)}), bf16[1024,1024]{1,0:T(8,128)(2,1)}) %all-gather.6.cloned.1.call-update) | async-done | bytes 2097168 | tf_op jit(solution)/shard_map/all_gather | solution.py:99
  129.2 2.1 convolution_convert_fusion.4
  131.3 1.5 collective-permute-start
  132.8 12.8 %collective-permute-done = bf16[192,1024]{1,0:T(8,128)(2,1)S(1)} collective-permute-done((bf16[192,1024]{1,0:T(8,128)(2,1)S(1)}, bf16[192,1024]{1,0:T(8,128)(2,1)S(1)}, u32[]{:S(2)}, u32[]{:S(2)}) %collective-permute-start) | collective-permute-done | bytes 393248 | tf_op jit(solution)/shard_map/ppermute | solution.py:130
  145.6 13.3 %collective-permute-done.1 = bf16[192,1024]{1,0:T(8,128)(2,1)S(1)} collective-permute-done((bf16[192,1024]{1,0:T(8,128)(2,1)S(1)}, bf16[192,1024]{1,0:T(8,128)(2,1)S(1)}, u32[]{:S(2)}, u32[]{:S(2)}) %collective-permute-start.1) | collective-permute-done | bytes 393248 | tf_op jit(solution)/shard_map/ppermute | solution.py:130
  159.0 14.3 %collective-permute-done.2 = bf16[192,1024]{1,0:T(8,128)(2,1)S(1)} collective-permute-done((bf16[192,1024]{1,0:T(8,128)(2,1)S(1)}, bf16[192,1024]{1,0:T(8,128)(2,1)S(1)}, u32[]{:S(2)}, u32[]{:S(2)}) %collective-permute-start.2) | collective-permute-done | bytes 393248 | tf_op jit(solution)/shard_map/ppermute | solution.py:130
  173.3 10.5 %collective-permute-done.3 = bf16[192,1024]{1,0:T(8,128)(2,1)S(1)} collective-permute-done((bf16[192,1024]{1,0:T(8,128)(2,1)S(1)}, bf16[192,1024]{1,0:T(8,128)(2,1)S(1)}, u32[]{:S(2)}, u32[]{:S(2)}) %collective-permute-start.3) | collective-permute-done | bytes 393248 | tf_op jit(solution)/shard_map/ppermute | solution.py:130
  184.5 6.0 all-to-all-start.2
  192.3 7.6 collective-permute-done.4
  202.6 10.1 %collective-permute-done.5 = bf16[192,1024]{1,0:T(8,128)(2,1)S(1)} collective-permute-done((bf16[192,1024]{1,0:T(8,128)(2,1)S(1)}, bf16[192,1024]{1,0:T(8,128)(2,1)S(1)}, u32[]{:S(2)}, u32[]{:S(2)}) %collective-permute-start.5) | collective-permute-done | bytes 393248 | tf_op jit(solution)/shard_map/ppermute | solution.py:130
  212.8 11.8 %all-reduce = s32[1536]{0:T(1024)S(1)} all-reduce(s32[1536]{0:T(1024)S(1)} %add_dynamic-update-slice_fusion), channel_id=1, replica_groups=mesh['fsdp'=4,'tok'=8] {'tok'}, use_global_device_ids=true, to_apply=%add | all-reduce | flops 1536 | bytes 12288
  225.2 2.1 convolution_convert_fusion.3
  228.2 1.7 copy.39
  232.0 2.6 constant_dynamic-slice_fusion.2
  234.6 34.2 %all-gather.12.cloned.1.call-done = bf16[1536,1024]{1,0:T(8,128)(2,1)} async-done(((bf16[192,1024]{1,0:T(8,128)(2,1)}), bf16[1536,1024]{1,0:T(8,128)(2,1)}) %all-gather.12.cloned.1.call-update) | async-done | bytes 3145744 | tf_op jit(solution)/shard_map/all_gather | solution.py:134
  268.8 607.9 %while.15 = (s32[]{:T(128)}, f32[64,16,64]{0,2,1:T(8,128)}, f32[16,64]{1,0:T(8,128)S(1)}, f32[16,64]{1,0:T(8,128)S(1)}, s32[64]{0:T(128)S(1)}, /*index=5*/s32[4,...) while((s32[]{:T(128)}, f32[64,16,64]{0,2,1:T(8,128)}, ...), condition=%wide.region_8.9_spmd.clone, body=%wide.region_5.8_spmd.clone.sunk | while | flops 183465984 | bytes 26422740 | solution.py:160
  269.6 135.5 %gather_fusion = s32[24576]{0:T(1024)S(1)} fusion(s32[1536]{0:T(1024)S(1)} %get-tuple-element.335, s32[24576]{0:T(1024)S(1)} %broadcast_clamp_fusion.2), kind=kCustom, calls=%fused_computation.clone.clone.1 | custom fusion | bytes 294912 | tf_op jit(solution)/shard_map/while/body/eval_jaxpr/jit(_take)/gather | solution.py:31
  405.9 1.8 fusion.71
  407.7 1.7 fusion.72
  409.5 2.4 constant_dynamic-slice_fusion.4
  413.1 4.1 select_reduce_fusion.5
  417.9 1.5 copy.52
  421.6 135.5 %gather_fusion = s32[24576]{0:T(1024)S(1)} fusion(s32[1536]{0:T(1024)S(1)} %get-tuple-element.335, s32[24576]{0:T(1024)S(1)} %broadcast_clamp_fusion.2), kind=kCustom, calls=%fused_computation.clone.clone.1 | custom fusion | bytes 294912 | tf_op jit(solution)/shard_map/while/body/eval_jaxpr/jit(_take)/gather | solution.py:31
  557.9 1.8 fusion.71
  559.7 1.7 fusion.72
  561.5 2.4 constant_dynamic-slice_fusion.4
  565.1 4.1 select_reduce_fusion.5
  569.8 1.5 copy.52
  573.6 135.5 %gather_fusion = s32[24576]{0:T(1024)S(1)} fusion(s32[1536]{0:T(1024)S(1)} %get-tuple-element.335, s32[24576]{0:T(1024)S(1)} %broadcast_clamp_fusion.2), kind=kCustom, calls=%fused_computation.clone.clone.1 | custom fusion | bytes 294912 | tf_op jit(solution)/shard_map/while/body/eval_jaxpr/jit(_take)/gather | solution.py:31
  709.8 1.8 fusion.71
  711.6 1.7 fusion.72
  713.4 2.4 constant_dynamic-slice_fusion.4
  717.1 4.1 select_reduce_fusion.5
  721.8 1.5 copy.52
  725.5 135.5 %gather_fusion = s32[24576]{0:T(1024)S(1)} fusion(s32[1536]{0:T(1024)S(1)} %get-tuple-element.335, s32[24576]{0:T(1024)S(1)} %broadcast_clamp_fusion.2), kind=kCustom, calls=%fused_computation.clone.clone.1 | custom fusion | bytes 294912 | tf_op jit(solution)/shard_map/while/body/eval_jaxpr/jit(_take)/gather | solution.py:31
  861.8 1.8 fusion.71
  863.6 1.7 fusion.72
  865.4 2.4 constant_dynamic-slice_fusion.4
  869.0 4.1 select_reduce_fusion.5
  873.8 1.5 copy.52
  877.8 2.2 fusion.25
  880.0 10.4 %all_to_all.25 = bf16[8,8,1024]{2,1,0:T(8,128)(2,1)S(1)} all-to-all(bf16[8,8,1024]{2,1,0:T(8,128)(2,1)S(1)} %fusion.25), channel_id=1, replica_groups=mesh['fsdp'=4,'tok'=8] {'tok'}, dimensions={0} | all-to-all | bytes 262144 | tf_op jit(solution)/shard_map/all_to_all | solution.py:173
  (176 shorter events, 37.4 us)
Async XLA Ops:
  7.2 11.9 %copy-start = (bf16[1,64,1024]{2,1,0:T(8,128)(2,1)S(1)}, bf16[1,64,1024]{2,1,0:T(8,128)(2,1)}, u32[]{:S(2)}) copy-start(bf16[1,64,1024]{2,1,0:T(8,128)(2,1)} %param.14) | copy-start | bytes 393220
  7.2 66.4 %copy-start.8 = (bf16[1,128,1024]{2,1,0:T(8,128)(2,1)S(1)}, bf16[1,128,1024]{2,1,0:T(8,128)(2,1)}, u32[]{:S(2)}) copy-start(bf16[1,128,1024]{2,1,0:T(8,128)(2,1)} %param.16) | copy-start | bytes 786436
  7.2 63.6 %all-gather.10.cloned.1.call-start = ((), (), s32[]{:S(2)}) async-start(), calls=%async_computation.6 | async-start | bytes 2162688 | tf_op jit(solution)/shard_map/all_gather | solution.py:100
  7.9 121.3 %all-gather.6.cloned.1.call-start = ((), (), s32[]{:S(2)}) async-start(), calls=%async_computation.4 | async-start | bytes 2162688 | tf_op jit(solution)/shard_map/all_gather | solution.py:99
  8.7 216.6 %all-gather.8.cloned.1.call-start = ((), (), s32[]{:S(2)}) async-start(), calls=%async_computation.5 | async-start | bytes 2162688 | tf_op jit(solution)/shard_map/all_gather | solution.py:98
  10.3 15.1 %copy-start.17 = (s32[64]{0:T(128)}, s32[64]{0:T(128)S(1)}, u32[]{:S(2)}) copy-start(s32[64]{0:T(128)S(1)} %convert_reduce_fusion) | copy-start | bytes 772
  11.8 13.7 %all-to-all-start = ((s32[8,1,8]{2,1,0:T(1,128)}), s32[8,1,8]{2,1,0:T(1,128)S(1)}, u32[]{:S(2)}, u32[]{:S(2)}) async-start(s32[8,1,8]{2,1,0:T(1,128)} %bitcast.1), calls=%async_computation | async-start | bytes 8192 | tf_op jit(solution)/shard_map/all_to_all | solution.py:90
  25.5 10.8 %all-to-all-start.1 = ((bf16[8,8,1024]{2,1,0:T(8,128)(2,1)}), bf16[8,8,1024]{2,1,0:T(8,128)(2,1)S(1)}, u32[]{:S(2)}, u32[]{:S(2)}) async-start(bf16[8,8,1024]{2,1,0:T(8,128)(2,1)} %fusion.26), calls=%async_computation.1 | async-start | bytes 262144 | tf_op jit(solution)/shard_map/all_to_all | solution.py:89
  28.8 239.9 %all-gather.12.cloned.1.call-start = ((), (), s32[]{:S(2)}) async-start(), calls=%async_computation.7 | async-start | bytes 3538944 | tf_op jit(solution)/shard_map/all_gather | solution.py:134
  29.0 173.5 %copy-start.15 = (s32[64]{0:T(128)}, s32[64]{0:T(128)S(1)}, u32[]{:S(2)}) copy-start(s32[64]{0:T(128)S(1)} %sub.73) | copy-start | bytes 772
  36.5 0.7 copy-start.5
  37.2 94.1 %copy-start.4 = (bf16[1,128,1024]{2,1,0:T(8,128)(2,1)S(1)}, bf16[1,128,1024]{2,1,0:T(8,128)(2,1)}, u32[]{:S(2)}) copy-start(bf16[1,128,1024]{2,1,0:T(8,128)(2,1)} %param.15) | copy-start | bytes 786436
  38.0 153.7 %copy-start.14 = (f32[32,16]{0,1:T(8,128)S(1)}, f32[32,16]{0,1:T(8,128)}, u32[]{:S(2)}) copy-start(f32[32,16]{0,1:T(8,128)} %param.20) | copy-start | bytes 6148
  38.0 161.9 %copy-start.19 = (u32[32]{0:T(128)S(1)}, u32[32]{0:T(128)}, u32[]{:S(2)}) copy-start(u32[32]{0:T(128)} %constant.86) | copy-start | bytes 388
  72.9 0.7 copy-start.7
  131.3 100.6 %copy-start.6 = (bf16[64,1024]{1,0:T(8,128)(2,1)}, bf16[64,1024]{1,0:T(8,128)(2,1)S(1)}, u32[]{:S(2)}) copy-start(bf16[64,1024]{1,0:T(8,128)(2,1)S(1)} %convolution_convert_fusion.4) | copy-start | bytes 393220
  131.3 14.3 %collective-permute-start = (bf16[192,1024]{1,0:T(8,128)(2,1)S(1)}, bf16[192,1024]{1,0:T(8,128)(2,1)S(1)}, u32[]{:S(2)}, u32[]{:S(2)}) collective-permute-start(bf16[192,1024]{1,0:T(8,128)(2,1)S(1)} %pad_maximum_fusion), channel_id=1, source_target_pairs={{0,1},{1,2},{2,3},{3,4},{4,5},{5,6},{6,7},{7,0},{8,9},{9,10},{10,1... | collective-permute-start | bytes 1179656 | tf_op jit(solution)/shard_map/ppermute | solution.py:130
  145.6 13.3 %collective-permute-start.1 = (bf16[192,1024]{1,0:T(8,128)(2,1)S(1)}, bf16[192,1024]{1,0:T(8,128)(2,1)S(1)}, u32[]{:S(2)}, u32[]{:S(2)}) collective-permute-start(bf16[192,1024]{1,0:T(8,128)(2,1)S(1)} %collective-permute-done), channel_id=1, source_target_pairs={{0,1},{1,2},{2,3},{3,4},{4,5},{5,6},{6,7},{7,0},{8,9},{9,10},{10,1... | collective-permute-start | bytes 1179656 | tf_op jit(solution)/shard_map/ppermute | solution.py:130
  159.0 14.3 %collective-permute-start.2 = (bf16[192,1024]{1,0:T(8,128)(2,1)S(1)}, bf16[192,1024]{1,0:T(8,128)(2,1)S(1)}, u32[]{:S(2)}, u32[]{:S(2)}) collective-permute-start(bf16[192,1024]{1,0:T(8,128)(2,1)S(1)} %collective-permute-done.1), channel_id=1, source_target_pairs={{0,1},{1,2},{2,3},{3,4},{4,5},{5,6},{6,7},{7,0},{8,9},{9,10},{10,1... | collective-permute-start | bytes 1179656 | tf_op jit(solution)/shard_map/ppermute | solution.py:130
  173.3 10.5 %collective-permute-start.3 = (bf16[192,1024]{1,0:T(8,128)(2,1)S(1)}, bf16[192,1024]{1,0:T(8,128)(2,1)S(1)}, u32[]{:S(2)}, u32[]{:S(2)}) collective-permute-start(bf16[192,1024]{1,0:T(8,128)(2,1)S(1)} %collective-permute-done.2), channel_id=1, source_target_pairs={{0,1},{1,2},{2,3},{3,4},{4,5},{5,6},{6,7},{7,0},{8,9},{9,10},{10,1... | collective-permute-start | bytes 1179656 | tf_op jit(solution)/shard_map/ppermute | solution.py:130
  183.8 16.1 %collective-permute-start.4 = (bf16[192,1024]{1,0:T(8,128)(2,1)S(1)}, bf16[192,1024]{1,0:T(8,128)(2,1)S(1)}, u32[]{:S(2)}, u32[]{:S(2)}) collective-permute-start(bf16[192,1024]{1,0:T(8,128)(2,1)S(1)} %collective-permute-done.3), channel_id=1, source_target_pairs={{0,1},{1,2},{2,3},{3,4},{4,5},{5,6},{6,7},{7,0},{8,9},{9,10},{10,1... | collective-permute-start | bytes 1179656 | tf_op jit(solution)/shard_map/ppermute | solution.py:130
  184.5 16.7 %all-to-all-start.2 = ((s32[8,1,8]{2,1,0:T(1,128)}), s32[8,1,8]{2,1,0:T(1,128)S(1)}, u32[]{:S(2)}, u32[]{:S(2)}) async-start(s32[8,1,8]{2,1,0:T(1,128)} %bitcast.6), calls=%async_computation.2 | async-start | bytes 8192 | tf_op jit(solution)/shard_map/all_to_all | solution.py:91
  190.5 687.3 %all-gather.14.cloned.1.call-start = ((), (), s32[]{:S(2)}) async-start(), calls=%async_computation.8 | async-start | bytes 2162688 | tf_op jit(solution)/shard_map/all_gather | solution.py:101
  199.9 12.8 %collective-permute-start.5 = (bf16[192,1024]{1,0:T(8,128)(2,1)S(1)}, bf16[192,1024]{1,0:T(8,128)(2,1)S(1)}, u32[]{:S(2)}, u32[]{:S(2)}) collective-permute-start(bf16[192,1024]{1,0:T(8,128)(2,1)S(1)} %collective-permute-done.4), channel_id=1, source_target_pairs={{0,1},{1,2},{2,3},{3,4},{4,5},{5,6},{6,7},{7,0},{8,9},{9,10},{10,1... | collective-permute-start | bytes 1179656 | tf_op jit(solution)/shard_map/ppermute | solution.py:130
  202.6 22.6 %copy-start.12 = (s32[64]{0:T(128)}, s32[64]{0:T(128)S(1)}, u32[]{:S(2)}) copy-start(s32[64]{0:T(128)S(1)} %broadcast_add_fusion.1) | copy-start | bytes 772
  212.7 18.6 %collective-permute-start.6 = (bf16[192,1024]{1,0:T(8,128)(2,1)S(1)}, bf16[192,1024]{1,0:T(8,128)(2,1)S(1)}, u32[]{:S(2)}, u32[]{:S(2)}) collective-permute-start(bf16[192,1024]{1,0:T(8,128)(2,1)S(1)} %collective-permute-done.5), channel_id=1, source_target_pairs={{0,1},{1,2},{2,3},{3,4},{4,5},{5,6},{6,7},{7,0},{8,9},{9,10},{10,1... | collective-permute-start | bytes 1179656 | tf_op jit(solution)/shard_map/ppermute | solution.py:130
  231.9 36.8 %copy-start.1 = (s32[1536]{0:T(1024)S(1)}, s32[1536]{0:T(1024)}, u32[]{:S(2)}) copy-start(s32[1536]{0:T(1024)} %param.19) | copy-start | bytes 18436
  231.9 36.8 %copy-start.9 = (bf16[32,16]{0,1:T(8,128)(2,1)S(1)}, bf16[32,16]{0,1:T(8,128)(2,1)}, u32[]{:S(2)}) copy-start(bf16[32,16]{0,1:T(8,128)(2,1)} %get-tuple-element.308) | copy-start | bytes 3076
  231.9 36.8 %copy-start.10 = (bf16[32,16]{0,1:T(8,128)(2,1)S(1)}, bf16[32,16]{0,1:T(8,128)(2,1)}, u32[]{:S(2)}) copy-start(bf16[32,16]{0,1:T(8,128)(2,1)} %get-tuple-element.307) | copy-start | bytes 3076
  232.0 36.8 %copy-start.11 = (bf16[32,16]{0,1:T(8,128)(2,1)S(1)}, bf16[32,16]{0,1:T(8,128)(2,1)}, u32[]{:S(2)}) copy-start(bf16[32,16]{0,1:T(8,128)(2,1)} %get-tuple-element.306) | copy-start | bytes 3076
  232.0 36.8 %copy-start.13 = (s32[64]{0:T(128)S(1)}, s32[64]{0:T(128)}, u32[]{:S(2)}) copy-start(s32[64]{0:T(128)} %copy-done.12) | copy-start | bytes 772
  268.8 609.0 %copy-start.16 = (s32[64]{0:T(128)S(1)}, s32[64]{0:T(128)}, u32[]{:S(2)}) copy-start(s32[64]{0:T(128)} %copy-done.15) | copy-start | bytes 772
  417.2 2.1 copy-start.2
  419.9 0.8 copy-start.3
  569.2 2.1 copy-start.2
  571.9 0.8 copy-start.3
  721.2 2.1 copy-start.2
  723.9 0.8 copy-start.3
  873.1 2.1 copy-start.2
  875.8 0.8 copy-start.3
  876.6 13.8 %copy-start.18 = (s32[64]{0:T(128)S(1)}, s32[64]{0:T(128)}, u32[]{:S(2)}) copy-start(s32[64]{0:T(128)} %copy-done.17) | copy-start | bytes 772
Sparse Core Ops, SparseCore 0:
  11.0 59.7 all-gather.9
  73.8 55.3 all-gather.5
  132.2 68.8 all-gather.7
  203.1 65.6 all-gather.11
  271.5 55.1 all-gather.13
